TPU v7x, 512 devices: a whole 4x8x8 slice. The times are simulated.
512 devices in a mesh: rep: 4 (over z_hi), fsdp: 128 (over z_lo, y, x, core).
Axes of the slice: x: 4, y: 8, z: 8 (z_hi: 4, z_lo: 2; z = z_hi * 2 + z_lo), core: 2. Of those that a mesh axis runs over, the one named last changes fastest.
Arguments:
- hidden: bfloat16 [4, 32768, 128], P('rep', 'fsdp'), may hold values from -4 to 4
- cotangent: bfloat16 [4, 32768, 8192], P('rep', 'fsdp'), may hold values from -0.0625 to 0.0625
- master: float32 [4, 128, 8192], P('rep', 'fsdp'), may hold values from -6 to 6
- adam_m: float32 [4, 128, 8192], P('rep', 'fsdp'), may hold values from -0.3125 to 0.3125
- adam_v: float32 [4, 128, 8192], P('rep', 'fsdp'), may hold values from 0.0005 to 0.008
- anchor: float32 [128, 8192], P('fsdp'), may hold values from -6 to 6
- outer_mom: float32 [128, 8192], P('fsdp'), may hold values from -1.75 to 1.75
- next_hidden: bfloat16 [4, 4096, 128], P('rep', 'fsdp'), may hold values from -0.5 to 0.5
Outputs:
- grad_hidden: bfloat16 [4, 32768, 128], P('rep', 'fsdp')
- merged: float32 [4, 128, 8192], P('rep', 'fsdp')
- new_anchor: float32 [128, 8192], P('fsdp')
- new_momentum: float32 [128, 8192], P('fsdp')
- next_out: bfloat16 [4, 4096, 8192], P('rep', 'fsdp')
All inputs are finite; a program needn't handle non-finite values.
Results may differ from a plain program's by a relative error of at most 0.018.
Values may be sent and summed in bfloat16 or wider, within the bound.
A program may use at most 64 MiB of HBM per device.

v0:
```python
import math
import jax
import jax.numpy as jnp
from jax import lax
from jax.sharding import PartitionSpec as P

BETA_ONE = 0.9
BETA_TWO = 0.95
INNER_LR = 0.3
DECAY = 0.1
EPS = 1e-08
OUTER_LR = 0.7
MOMENTUM = 0.9
ALPHA = 0.5
STEP = 100


def hadamard_table():
    index = jnp.arange(128, dtype=jnp.int32)
    count = jnp.zeros((128, 128), jnp.int32)
    for bit in range(7):
        left = jnp.bitwise_and(jnp.right_shift(index, bit), 1)
        count = count + left[:, None] * left[None, :]
    return (1 - 2 * (count % 2)).astype(jnp.float32)


def sign_vector(width):
    index = jnp.arange(width, dtype=jnp.int32)
    return (1 - 2 * (index * 97 % 251 % 2)).astype(jnp.float32)


def block_rotate(values, table):
    rows, width = values.shape
    blocks = values.reshape(rows, width // 128, 128)
    out = jnp.einsum("rbk,kj->rbj", blocks, table, precision=lax.Precision.HIGHEST)
    return out.reshape(rows, width) * (1.0 / math.sqrt(128.0))


def shards(hidden, cotangent, master, adam_m, adam_v, anchor, outer_mom, next_hidden):
    table = hadamard_table()
    width = master.shape[2]
    hidden_rows = hidden[0]
    cotangent_rows = cotangent[0]
    weights16 = master[0].astype(jnp.bfloat16)
    all_weights = lax.all_gather(weights16, "fsdp", axis=0, tiled=True)
    grad_hidden = lax.dot_general(
        cotangent_rows, all_weights, (((1,), (1,)), ((), ())), preferred_element_type=jnp.float32
    ).astype(jnp.bfloat16)
    full_grad = lax.dot_general(
        hidden_rows, cotangent_rows, (((0,), (0,)), ((), ())), preferred_element_type=jnp.float32
    )
    gradient = lax.psum_scatter(full_grad, "fsdp", scatter_dimension=0, tiled=True)
    corr_one = 1.0 - BETA_ONE**STEP
    corr_two = 1.0 - BETA_TWO**STEP
    first = BETA_ONE * adam_m[0] + (1.0 - BETA_ONE) * gradient
    second = BETA_TWO * adam_v[0] + (1.0 - BETA_TWO) * gradient * gradient
    update = first / corr_one / (jnp.sqrt(second / corr_two) + EPS) + DECAY * master[0]
    inner = master[0] - INNER_LR * update
    signs = sign_vector(width)
    rotated = block_rotate((anchor - inner) * signs[None, :], table).astype(jnp.bfloat16)
    replicas = lax.axis_size("rep")
    total = lax.psum(rotated.astype(jnp.float32).astype(jnp.bfloat16), "rep").astype(jnp.float32)
    mean_delta = block_rotate(total, table) * signs[None, :] / replicas
    new_momentum = MOMENTUM * outer_mom + mean_delta
    new_anchor = anchor - OUTER_LR * (MOMENTUM * new_momentum + mean_delta)
    merged = ALPHA * inner + (1.0 - ALPHA) * new_anchor
    merged16 = merged.astype(jnp.bfloat16)
    next_rows = next_hidden[0]
    all_merged = lax.all_gather(merged16, "fsdp", axis=0, tiled=True)
    next_out = jnp.dot(next_rows, all_merged, preferred_element_type=jnp.float32).astype(
        jnp.bfloat16
    )
    return (grad_hidden[None], merged[None], new_anchor, new_momentum, next_out[None])


def solution(mesh):
    in_specs = (
        P("rep", "fsdp", None),
        P("rep", "fsdp", None),
        P("rep", "fsdp", None),
        P("rep", "fsdp", None),
        P("rep", "fsdp", None),
        P("fsdp", None),
        P("fsdp", None),
        P("rep", "fsdp", None),
    )
    out_specs = (
        P("rep", "fsdp", None),
        P("rep", "fsdp", None),
        P("fsdp", None),
        P("fsdp", None),
        P("rep", "fsdp", None),
    )
    return jax.shard_map(shards, mesh=mesh, in_specs=in_specs, out_specs=out_specs, check_vma=False)
```

profile of v0, /device:TPU:8, one launch (start us, length us, event | category | flops | bytes accessed | tf_op | source)
XLA Modules:
  0.0 1570.5 jit_solution(18300237138548457707)
XLA Ops:
  7.2 0.0 copy-start
  7.2 0.0 all-reduce.3.cloned.1.call-start
  7.2 0.8 copy-done
  8.0 4.9 fusion.1
  12.9 0.0 copy-start.3
  12.9 0.0 copy-start.1
  12.9 0.0 copy-start.4
  12.9 0.0 copy-start.5
  12.9 0.0 copy-start.6
  12.9 0.0 all-reduce.3.cloned.1.call-update
  13.0 0.0 all-gather.5.cloned.1.call-start
  13.0 0.7 copy-done.3
  13.7 0.6 fusion.32
  14.3 0.0 all-gather.5.cloned.1.call-update
  14.3 0.0 all-gather.7.cloned.1.call-start
  14.4 1.3 dynamic-slice
  15.7 1087.4 %all-reduce.3.cloned.1.call-done = f32[128,8192]{1,0:T(8,128)} async-done(((f32[128,8192]{1,0:T(8,128)}), f32[128,8192]{1,0:T(8,128)}) %all-reduce.3.cloned.1.call-update) | async-done | bytes 4194320
  1103.1 0.0 copy-done.1
  1103.1 0.0 copy-done.4
  1103.1 0.0 copy-done.5
  1103.1 2.1 subtract_multiply_fusion
  1105.2 0.0 copy-start.7
  1105.2 0.4 fusion.19
  1105.6 19.6 %psum.7 = bf16[64,128]{1,0:T(8,128)(2,1)S(1)} all-reduce(bf16[64,128]{1,0:T(8,128)(2,1)S(1)} %fusion.19), channel_id=1, replica_groups=mesh['rep'=4,'fsdp'=128] {'rep'}, use_global_device_ids=true, to_apply=%region_1.2 | all-reduce | flops 8192 | bytes 32768 | tf_op jit(solution)/shard_map/psum | solution.py:62
  1125.2 0.3 convolution_multiply_fusion
  1125.6 0.0 copy-done.6
  1125.6 1.0 convert_bitcast_fusion
  1126.6 0.0 copy-start.2
  1126.6 0.0 all-gather.7.cloned.1.call-update
  1126.6 211.1 %all-gather.5.cloned.1.call-done = bf16[128,1,8192]{2,1,0:T(2,128)(2,1)} async-done(((bf16[1,1,8192]{2,1,0:T(2,128)(2,1)}), bf16[128,1,8192]{2,1,0:T(2,128)(2,1)}) %all-gather.5.cloned.1.call-update) | async-done | bytes 2097168 | tf_op jit(solution)/shard_map/all_gather | solution.py:45
  1337.7 7.0 fusion.14
  1344.7 0.7 fusion.44
  1345.3 213.2 %all-gather.7.cloned.1.call-done = bf16[128,1,8192]{2,1,0:T(2,128)(2,1)} async-done(((bf16[1,1,8192]{2,1,0:T(2,128)(2,1)}), bf16[128,1,8192]{2,1,0:T(2,128)(2,1)}) %all-gather.7.cloned.1.call-update) | async-done | bytes 2097168 | tf_op jit(solution)/shard_map/all_gather | solution.py:69
  1558.5 0.0 copy-done.7
  1558.6 5.4 fusion
  1564.0 0.0 copy-done.2
  (4 shorter events, 0.0 us)
Async XLA Ops:
  7.2 0.8 copy-start
  7.2 1095.9 %all-reduce.3.cloned.1.call-start = ((), (), s32[]{:S(2)}) async-start(), calls=%async_computation.2 | async-start | bytes 8388608
  12.9 0.8 copy-start.3
  12.9 1090.2 %copy-start.1 = (f32[1,8192]{1,0:T(1,128)S(1)}, f32[1,8192]{1,0:T(1,128)}, u32[]{:S(2)}) copy-start(f32[1,8192]{1,0:T(1,128)} %param.13) | copy-start | bytes 98308
  12.9 1090.2 %copy-start.4 = (f32[1,1,8192]{2,1,0:T(1,128)S(1)}, f32[1,1,8192]{2,1,0:T(1,128)}, u32[]{:S(2)}) copy-start(f32[1,1,8192]{2,1,0:T(1,128)} %param.12) | copy-start | bytes 98308
  12.9 1090.2 %copy-start.5 = (f32[1,1,8192]{2,1,0:T(1,128)S(1)}, f32[1,1,8192]{2,1,0:T(1,128)}, u32[]{:S(2)}) copy-start(f32[1,1,8192]{2,1,0:T(1,128)} %param.11) | copy-start | bytes 98308
  12.9 1112.6 %copy-start.6 = (f32[1,8192]{1,0:T(1,128)S(1)}, f32[1,8192]{1,0:T(1,128)}, u32[]{:S(2)}) copy-start(f32[1,8192]{1,0:T(1,128)} %param.14) | copy-start | bytes 98308
  13.0 1324.7 %all-gather.5.cloned.1.call-start = ((), (), s32[]{:S(2)}) async-start(), calls=%async_computation | async-start | bytes 4227072 | tf_op jit(solution)/shard_map/all_gather | solution.py:45
  14.3 1544.2 %all-gather.7.cloned.1.call-start = ((), (), s32[]{:S(2)}) async-start(), calls=%async_computation.1 | async-start | bytes 4227072 | tf_op jit(solution)/shard_map/all_gather | solution.py:69
  1105.2 453.3 %copy-start.7 = (bf16[1,32,128]{2,1,0:T(8,128)(2,1)S(1)}, bf16[1,32,128]{2,1,0:T(8,128)(2,1)}, u32[]{:S(2)}) copy-start(bf16[1,32,128]{2,1,0:T(8,128)(2,1)} %param.15) | copy-start | bytes 24580
  1126.6 437.4 %copy-start.2 = (f32[1,8192]{1,0:T(1,128)}, f32[1,8192]{1,0:T(1,128)S(1)}, u32[]{:S(2)}) copy-start(f32[1,8192]{1,0:T(1,128)S(1)} %get-tuple-element.6) | copy-start | bytes 98308
Sparse Core Ops, SparseCore 0:
  13.1 1089.9 all-reduce.2
  1106.1 231.5 all-gather.4
  1340.7 217.8 all-gather.6
where the time goes:
time: 1570 us
  waiting for transfers between devices  1510 us (96%)
  blocking collectives  19.6 us (1%)
  matrix products  18 us (1%)
    unnamed x4, waiting for transfers between devices  1090 us
    all_gather x1, waiting for transfers between devices, shards(): all_merged = lax.all_gather(merged16, 'fsdp', axis=0, tiled=True)  213 us
    all_gather x1, waiting for transfers between devices, shards(): all_weights = lax.all_gather(weights16, 'fsdp', axis=0, tiled=True)  211 us
  transfers between devices with their start and end apart: 3, of which 3 were waited for; matrix products, arithmetic and copies ran while one was open for 1% of the time, Pallas kernels for 0%

commit v1 on v0

--- a/solution.py
+++ b/solution.py
@@ -66,7 +66,9 @@
     merged = ALPHA * inner + (1.0 - ALPHA) * new_anchor
     merged16 = merged.astype(jnp.bfloat16)
     next_rows = next_hidden[0]
-    all_merged = lax.all_gather(merged16, "fsdp", axis=0, tiled=True)
+    all_merged = jnp.concatenate(
+        lax.all_to_all(jnp.stack([merged16] * lax.axis_size("fsdp")), "fsdp", 0, 0), axis=0
+    )
     next_out = jnp.dot(next_rows, all_merged, preferred_element_type=jnp.float32).astype(
         jnp.bfloat16
     )

time: 1570 us -> 1370 us (0.87)
  waiting for transfers between devices: 1510 us -> 1260 us
  starting transfers between devices: 0.12 us -> 25.2 us
  local copies, waits for them, and re-layouts: 2.75 us -> 18.9 us
    all_gather x1 -> x0, waiting for transfers between devices: 213 us -> none  [shards(): all_merged = lax.all_gather(merged16, 'fsdp', axis=0, tiled=True)]
    all_gather x1, waiting for transfers between devices: 211 us -> 172 us  [shards(): all_weights = lax.all_gather(weights16, 'fsdp', axis=0, tiled=True)]
    all_to_all x0 -> x1, starting transfers between devices: none -> 25.1 us  [shards(): lax.all_to_all(jnp.stack([merged16] * lax.axis_size('fsdp')), 'fsdp', 0, 0)]
    unnamed x4 -> x3, waiting for transfers between devices: 1090 us -> 1090 us
  transfers between devices with their start and end apart: 3 -> 3, of which waited for: 3 -> 2; matrix products, arithmetic and copies ran while one was open for 1% -> 3% of each run, Pallas kernels for 0% -> 0%
where the time goes in v1:
time: 1370 us
  waiting for transfers between devices  1260 us (92%)
  starting transfers between devices  25.2 us (2%)
  blocking collectives  19.6 us (1%)
  local copies, waits for them, and re-layouts  18.9 us (1%)
  matrix products  18 us (1%)
  other arithmetic  17.6 us (1%)
  between operations  14.2 us (1%)
    unnamed x3, waiting for transfers between devices  1090 us
    all_gather x1, waiting for transfers between devices, shards(): all_weights = lax.all_gather(weights16, 'fsdp', axis=0, tiled=True)  172 us
  transfers between devices with their start and end apart: 3, of which 2 were waited for; matrix products, arithmetic and copies ran while one was open for 3% of the time, Pallas kernels for 0%

profile of v1, /device:TPU:8, one launch (start us, length us, event | category | flops | bytes accessed | tf_op | source)
XLA Modules:
  0.0 1370.8 jit_solution(7404302678454090288)
XLA Ops:
  7.2 0.0 copy-start
  7.2 0.0 all-reduce.3.cloned.1.call-start
  7.2 0.8 copy-done
  8.0 4.9 fusion.1
  12.9 0.0 copy-start.1
  12.9 0.0 copy-start.2
  12.9 0.0 copy-start.4
  12.9 0.0 copy-start.5
  12.9 0.0 copy-start.6
  12.9 0.0 all-reduce.3.cloned.1.call-update
  13.0 0.0 all-gather.3.cloned.1.call-start
  13.0 0.7 copy-done.1
  13.7 0.6 fusion.32
  14.3 0.0 all-gather.3.cloned.1.call-update
  14.4 1.3 dynamic-slice
  15.7 1085.7 %all-reduce.3.cloned.1.call-done = f32[128,8192]{1,0:T(8,128)} async-done(((f32[128,8192]{1,0:T(8,128)}), f32[128,8192]{1,0:T(8,128)}) %all-reduce.3.cloned.1.call-update) | async-done | bytes 4194320
  1101.4 0.0 copy-done.2
  1101.4 0.0 copy-done.4
  1101.4 0.0 copy-done.5
  1101.4 2.1 subtract_multiply_fusion
  1103.5 0.4 fusion.19
  1103.9 19.6 %psum.7 = bf16[64,128]{1,0:T(8,128)(2,1)S(1)} all-reduce(bf16[64,128]{1,0:T(8,128)(2,1)S(1)} %fusion.19), channel_id=1, replica_groups=mesh['rep'=4,'fsdp'=128] {'rep'}, use_global_device_ids=true, to_apply=%region_1.2 | all-reduce | flops 8192 | bytes 32768 | tf_op jit(solution)/shard_map/psum | solution.py:62
  1123.5 0.3 convolution_multiply_fusion
  1123.8 0.0 copy-done.6
  1123.8 1.0 convert_reduce_fusion
  1124.8 0.0 copy-start.3
  1124.8 6.2 stack.2
  1131.0 0.5 broadcast.364
  1131.5 13.2 reduce.2
  1144.7 2.8 reshape.271
  1147.5 25.1 %all-to-all-start = ((bf16[128,2,4096]{2,1,0:T(2,128)(2,1)}), bf16[128,2,4096]{2,1,0:T(2,128)(2,1)S(1)}, u32[]{:S(2)}, u32[]{:S(2)}) async-start(bf16[128,2,4096]{2,1,0:T(2,128)(2,1)} %reshape.271), calls=%async_computation | async-start | bytes 4194304 | tf_op jit(solution)/shard_map/all_to_all | solution.py:70
  1172.6 171.5 %all-gather.3.cloned.1.call-done = bf16[128,1,8192]{2,1,0:T(2,128)(2,1)} async-done(((bf16[1,1,8192]{2,1,0:T(2,128)(2,1)}), bf16[128,1,8192]{2,1,0:T(2,128)(2,1)}) %all-gather.3.cloned.1.call-update) | async-done | bytes 2097168 | tf_op jit(solution)/shard_map/all_gather | solution.py:45
  1344.2 7.0 fusion.14
  1351.1 0.0 copy-start.7
  1351.1 0.0 copy-done.3
  1351.1 0.7 fusion.44
  1351.8 0.0 all-to-all-done
  1351.8 6.7 reshape.272
  1358.5 0.0 copy-done.7
  1358.5 5.4 fusion
  (4 shorter events, 0.0 us)
Async XLA Ops:
  7.2 0.8 copy-start
  7.2 1094.2 %all-reduce.3.cloned.1.call-start = ((), (), s32[]{:S(2)}) async-start(), calls=%async_computation.2 | async-start | bytes 8388608
  12.9 0.8 copy-start.1
  12.9 1088.5 %copy-start.2 = (f32[1,8192]{1,0:T(1,128)S(1)}, f32[1,8192]{1,0:T(1,128)}, u32[]{:S(2)}) copy-start(f32[1,8192]{1,0:T(1,128)} %param.13) | copy-start | bytes 98308
  12.9 1088.5 %copy-start.4 = (f32[1,1,8192]{2,1,0:T(1,128)S(1)}, f32[1,1,8192]{2,1,0:T(1,128)}, u32[]{:S(2)}) copy-start(f32[1,1,8192]{2,1,0:T(1,128)} %param.12) | copy-start | bytes 98308
  12.9 1088.5 %copy-start.5 = (f32[1,1,8192]{2,1,0:T(1,128)S(1)}, f32[1,1,8192]{2,1,0:T(1,128)}, u32[]{:S(2)}) copy-start(f32[1,1,8192]{2,1,0:T(1,128)} %param.11) | copy-start | bytes 98308
  12.9 1110.9 %copy-start.6 = (f32[1,8192]{1,0:T(1,128)S(1)}, f32[1,8192]{1,0:T(1,128)}, u32[]{:S(2)}) copy-start(f32[1,8192]{1,0:T(1,128)} %param.14) | copy-start | bytes 98308
  13.0 1331.2 %all-gather.3.cloned.1.call-start = ((), (), s32[]{:S(2)}) async-start(), calls=%async_computation.1 | async-start | bytes 4227072 | tf_op jit(solution)/shard_map/all_gather | solution.py:45
  1124.8 226.3 %copy-start.3 = (f32[1,8192]{1,0:T(1,128)}, f32[1,8192]{1,0:T(1,128)S(1)}, u32[]{:S(2)}) copy-start(f32[1,8192]{1,0:T(1,128)S(1)} %get-tuple-element.6) | copy-start | bytes 98308
  1147.5 204.3 %all-to-all-start = ((bf16[128,2,4096]{2,1,0:T(2,128)(2,1)}), bf16[128,2,4096]{2,1,0:T(2,128)(2,1)S(1)}, u32[]{:S(2)}, u32[]{:S(2)}) async-start(bf16[128,2,4096]{2,1,0:T(2,128)(2,1)} %reshape.271), calls=%async_computation | async-start | bytes 4194304 | tf_op jit(solution)/shard_map/all_to_all | solution.py:70
  1351.1 7.4 copy-start.7
Sparse Core Ops, SparseCore 0:
  13.1 1088.2 all-reduce.2
  1104.3 239.7 all-gather.2
